TPU v7x, 256 devices: a whole 4x4x8 slice. The times are simulated.
256 devices in a mesh: rows: 128 (over z, y, x), cols: 2 (over core).
Axes of the slice: x: 4, y: 4, z: 8, core: 2. Of those that a mesh axis runs over, the one named last changes fastest.
Arguments:
- design: float32 [131072, 512], P('rows', 'cols'), may hold values from -24 to 24
- signs: int32 [131072], P('rows'), may hold values from -1 to 1, as said below
- kept: int32 [8192], replicated, may hold values from 0 to 131071, as said below
Outputs:
- sketch: float32 [8192, 512], P('rows', 'cols')
- factor: float32 [512, 512], P(None, 'cols')
Inputs may be any that keep to these rules, and one draw needn't show every extreme that they name: `signs`: each entry is +1 or -1. `kept`: distinct and increasing.
All inputs are finite; a program needn't handle non-finite values.
Results may differ from a plain program's by a relative error of at most 0.0003.
Values sent between devices are 32-bit elements; how exact they have to be, the bound alone decides.
No kernel may reach another device: no remote copies, remote signals or barrier semaphores. Data moves between devices by JAX's collectives and lax.ppermute only.
A program may use at most 64 MiB of HBM per device.

v0:
```python
import math
import jax
import jax.numpy as jnp
from jax import lax
from jax.sharding import Mesh
from jax.sharding import PartitionSpec as P

ROWS = ("rows_0", "rows_1", "rows_2")


def sum_by_axis(so_far, axes):
    for axis in axes:
        so_far = lax.psum_scatter(so_far, axis, scatter_dimension=0, tiled=True)
    return so_far


def laid_out(parts, dim):
    dims = list(parts.shape[1:])
    dims[dim] *= parts.shape[0]
    return jnp.moveaxis(parts, 0, dim).reshape(dims)


def copy_for_each(shard, axis):
    length = lax.axis_size(axis)
    return lax.all_to_all(
        jnp.broadcast_to(shard[None], (length, *shard.shape)), axis, 0, 0, tiled=True
    )


def gathered_copies(shard, axis, dim):
    return laid_out(copy_for_each(shard, axis), dim)


def hadamard(order):
    matrix = jnp.ones((1, 1), jnp.float32)
    base = jnp.array([[1.0, 1.0], [1.0, -1.0]], jnp.float32)
    while matrix.shape[0] < order:
        matrix = jnp.kron(matrix, base)
    return matrix


def bit_parity(value):
    folded = value
    for amount in (16, 8, 4, 2, 1):
        folded = jnp.bitwise_xor(folded, jnp.right_shift(folded, amount))
    return jnp.bitwise_and(folded, 1)


def local_transform(flipped):
    length, width = flipped.shape
    outer = length // 128
    inner_table = hadamard(128)
    outer_table = hadamard(outer)
    blocks = flipped.reshape(outer, 128, width)
    mixed = jnp.einsum("pb,abc->apc", inner_table, blocks, precision=lax.Precision.HIGHEST)
    mixed = jnp.einsum("qa,apc->qpc", outer_table, mixed, precision=lax.Precision.HIGHEST)
    return mixed.reshape(length, width)


def signed_rows(transformed, kept_part, device_row, total_rows):
    length = transformed.shape[0]
    kept_blocks = kept_part // length
    offsets = kept_part - kept_blocks * length
    parity = bit_parity(jnp.bitwise_and(kept_blocks, device_row))
    factor = (1.0 - 2.0 * parity.astype(jnp.float32)) / math.sqrt(total_rows)
    return jnp.take(transformed, offsets, axis=0) * factor[:, None]


def body(design, signs, kept):
    flipped = design * signs.astype(jnp.float32)[:, None]
    transformed = local_transform(flipped)
    device_row = lax.axis_index(ROWS)
    groups = lax.axis_size(ROWS)
    length = transformed.shape[0]
    widths = transformed.shape[1]
    total_rows = length * groups
    sketch = sum_by_axis(signed_rows(transformed, kept, device_row, total_rows), ROWS)
    column = lax.axis_index("cols")
    whole = gathered_copies(sketch, "cols", 1)
    kept_total = kept.shape[0]
    partial_gram = jnp.dot(
        whole.T, whole, precision=lax.Precision.HIGHEST, preferred_element_type=jnp.float32
    )
    gram = lax.psum(partial_gram, ROWS) / kept_total
    factor = jnp.linalg.cholesky(gram).T
    return (sketch, lax.dynamic_slice_in_dim(factor, column * widths, widths, 1))


def solution(mesh):
    torus = Mesh(
        mesh.devices.reshape(8, 4, 4, mesh.shape["cols"]), ("rows_0", "rows_1", "rows_2", "cols")
    )
    return jax.shard_map(
        body,
        mesh=torus,
        in_specs=(P(ROWS, "cols"), P(ROWS), P()),
        out_specs=(P(ROWS, "cols"), P(None, "cols")),
        check_vma=False,
    )
```

profile of v0, /device:TPU:2, one launch (start us, length us, event | category | flops | bytes accessed | tf_op | source)
XLA Modules:
  0.0 540.0 jit_solution(2784497924892284188)
XLA Ops:
  7.2 0.8 broadcast_multiply_fusion.7
  8.1 0.1 mul.255
  8.2 0.8 broadcast_multiply_fusion.6
  9.1 0.8 broadcast_clamp_fusion
  9.9 0.8 compare_and_fusion
  10.7 0.7 convert_element_type.6
  11.4 0.8 broadcast_multiply_fusion.5
  12.2 0.8 broadcast_multiply_fusion.4
  13.0 0.1 mul.277
  13.1 0.9 broadcast_multiply_fusion.2
  14.0 0.6 mul.281
  14.7 3.0 broadcast_multiply_fusion
  17.7 4.0 reshape.195
  21.7 0.2 broadcast_multiply_fusion.3
  21.9 1.8 convolution_bitcast_fusion
  23.7 0.5 copy.15
  24.2 1.0 fusion.21
  25.2 0.3 copy.16
  25.6 31.4 %gather_fusion = f32[8192,256]{1,0:T(8,128)} fusion(f32[1024,256]{1,0:T(8,128)S(1)} %bitcast.45, s32[8192]{0:T(1024)S(1)} %broadcast_clamp_fusion), kind=kCustom, calls=%fused_computation | custom fusion | bytes 16809984 | tf_op jit(solution)/shard_map/jit(_take)/gather | solution.py:66
  57.0 9.9 %select_multiply_fusion = f32[8192,256]{1,0:T(8,128)} fusion(f32[8192,256]{1,0:T(8,128)} %gather_fusion, f32[8192]{0:T(1024)S(1)} %fusion.19, pred[8192]{0:T(1024)(128)(4,1)S(1)} %compare_and_fusion), kind=kLoop, calls=%fused_computation.1 | loop fusion | flops 4194304 | bytes 16818176 | tf_op jit(solution)/shard_map/mul | solution.py:66
  66.9 97.9 %reduce-scatter.4.cloned.1.call-done = f32[1024,256]{1,0:T(8,128)} async-done(((f32[8192,256]{1,0:T(8,128)}), f32[1024,256]{1,0:T(8,128)}) %reduce-scatter.4.cloned.1.call-update) | async-done | bytes 1048592 | tf_op jit(solution)/shard_map/reduce_scatter | solution.py:13
  165.0 27.3 %reduce-scatter.6.cloned.1.call-done = f32[256,256]{1,0:T(8,128)} async-done(((f32[1024,256]{1,0:T(8,128)}), f32[256,256]{1,0:T(8,128)}) %reduce-scatter.6.cloned.1.call-update) | async-done | bytes 262160 | tf_op jit(solution)/shard_map/reduce_scatter | solution.py:13
  192.3 24.3 %reduce-scatter.8.cloned.1.call-done = f32[64,256]{1,0:T(8,128)} async-done(((f32[256,256]{1,0:T(8,128)}), f32[64,256]{1,0:T(8,128)}) %reduce-scatter.8.cloned.1.call-update) | async-done | bytes 65552 | tf_op jit(solution)/shard_map/reduce_scatter | solution.py:13
  216.6 0.8 broadcast_in_dim.59
  217.4 3.8 all_to_all.5
  221.3 2.1 fusion.22
  223.4 222.7 %all-reduce.3.cloned.1.call-done = f32[512,512]{0,1:T(8,128)} async-done(((f32[512,512]{0,1:T(8,128)}), f32[512,512]{0,1:T(8,128)}) %all-reduce.3.cloned.1.call-update) | async-done | bytes 1048592 | tf_op jit(solution)/shard_map/psum | solution.py:84
  446.1 1.3 broadcast_multiply_fusion.1
  447.4 0.3 copy.19
  447.7 1.5 fusion
  449.2 11.7 %cholesky.104 = f32[128,128]{1,0:T(8,128)S(1)} custom-call(f32[128,128]{1,0:T(8,128)S(1)} %cholesky.266), custom_call_target="Cholesky" | custom-call | tf_op jit(solution)/shard_map/jit(cholesky)/cholesky | solution.py:85
  461.0 0.1 cholesky.224
  461.1 9.8 %custom-call.27 = f32[1,128,128]{1,2,0:T(8,128)S(1)} custom-call(f32[1,128,128]{2,1,0:T(8,128)S(1)} %get-tuple-element.17), custom_call_target="InvertDiagBlocksLowerTriangular" | custom-call | tf_op jit(solution)/shard_map/jit(cholesky)/cholesky | solution.py:85
  470.9 0.3 constant_dynamic-update-slice_fusion.1
  471.2 0.3 convolution_subtract_fusion
  471.6 11.7 %cholesky.217 = f32[128,128]{1,0:T(8,128)S(1)} custom-call(f32[128,128]{1,0:T(8,128)S(1)} %cholesky.270), custom_call_target="Cholesky" | custom-call | tf_op jit(solution)/shard_map/jit(cholesky)/cholesky | solution.py:85
  483.3 9.9 %custom-call.28 = f32[1,128,128]{1,2,0:T(8,128)S(1)} custom-call(f32[1,128,128]{2,1,0:T(8,128)S(1)} %get-tuple-element.14), custom_call_target="InvertDiagBlocksLowerTriangular" | custom-call | tf_op jit(solution)/shard_map/jit(cholesky)/cholesky | solution.py:85
  493.3 0.3 convolution_dynamic-update-slice_fusion
  493.6 0.4 convolution_subtract_fusion.1
  494.0 11.7 %cholesky.238 = f32[128,128]{1,0:T(8,128)S(1)} custom-call(f32[128,128]{1,0:T(8,128)S(1)} %cholesky.275), custom_call_target="Cholesky" | custom-call | tf_op jit(solution)/shard_map/jit(cholesky)/cholesky | solution.py:85
  505.7 9.8 %custom-call.29 = f32[1,128,128]{1,2,0:T(8,128)S(1)} custom-call(f32[1,128,128]{2,1,0:T(8,128)S(1)} %get-tuple-element.11), custom_call_target="InvertDiagBlocksLowerTriangular" | custom-call | tf_op jit(solution)/shard_map/jit(cholesky)/cholesky | solution.py:85
  515.5 0.2 convolution_dynamic-update-slice_fusion.1
  515.7 0.4 convolution_subtract_fusion.2
  516.1 11.7 %cholesky.255 = f32[128,128]{1,0:T(8,128)S(1)} custom-call(f32[128,128]{1,0:T(8,128)S(1)} %convolution_subtract_fusion.2), custom_call_target="Cholesky" | custom-call | tf_op jit(solution)/shard_map/jit(cholesky)/cholesky | solution.py:85
  527.9 0.7 compare_reduce_fusion.1
  528.6 0.6 compare_reduce_fusion
  529.2 0.7 compare_reduce_fusion.2
  532.5 1.0 copy.20
  (25 shorter events, 0.8 us)
Async XLA Ops:
  7.2 14.5 %copy-start = (f32[1024,256]{1,0:T(8,128)S(1)}, f32[1024,256]{1,0:T(8,128)}, u32[]{:S(2)}) copy-start(f32[1024,256]{1,0:T(8,128)} %param.5) | copy-start | bytes 3145732
  7.2 157.7 %reduce-scatter.4.cloned.1.call-start = ((), (), s32[]{:S(2)}) async-start(), calls=%async_computation.4 | async-start | bytes 9437184 | tf_op jit(solution)/shard_map/reduce_scatter | solution.py:13
  17.7 7.9 %copy-start.1 = (s32[8192]{0:T(1024)S(1)}, s32[8192]{0:T(1024)}, u32[]{:S(2)}) copy-start(s32[8192]{0:T(1024)} %param.7) | copy-start | bytes 98308
  66.9 125.3 %reduce-scatter.6.cloned.1.call-start = ((), (), s32[]{:S(2)}) async-start(), calls=%async_computation.5 | async-start | bytes 1310720 | tf_op jit(solution)/shard_map/reduce_scatter | solution.py:13
  164.9 51.7 %reduce-scatter.8.cloned.1.call-start = ((), (), s32[]{:S(2)}) async-start(), calls=%async_computation.6 | async-start | bytes 327680 | tf_op jit(solution)/shard_map/reduce_scatter | solution.py:13
  192.3 253.8 %all-reduce.3.cloned.1.call-start = ((), (), s32[]{:S(2)}) async-start(), calls=%async_computation.7 | async-start | bytes 2097152 | tf_op jit(solution)/shard_map/psum | solution.py:84
Sparse Core Ops, SparseCore 0:
  67.0 97.8 reduce-scatter.3
  167.4 24.7 reduce-scatter.5
  195.5 21.0 reduce-scatter.7
  223.5 222.5 all-reduce.2
where the time goes:
time: 541 us; the launch traced here: 540 us
  waiting for transfers between devices  372 us (69%)
  other arithmetic  101 us (19%)
  local copies, waits for them, and re-layouts  39.6 us (7%)
  between operations  16.6 us (3%)
  matrix products  6.71 us (1%)
    psum x1, waiting for transfers between devices, body(): gram = lax.psum(partial_gram, ROWS) / kept_total  223 us
    reduce_scatter x3, waiting for transfers between devices, sum_by_axis(): so_far = lax.psum_scatter(so_far, axis, scatter_dimension=0, tiled=True)  149 us
    another operation x14, other arithmetic, body(): factor = jnp.linalg.cholesky(gram).T  78.6 us
    gather x1, local copies, waits for them, and re-layouts, signed_rows(): return jnp.take(transformed, offsets, axis=0) * factor[:, None]  31.4 us
  transfers between devices with their start and end apart: 4, of which 4 were waited for; matrix products, arithmetic and copies ran while one was open for 0% of the time, Pallas kernels for 0%

commit v1 on v0

--- a/solution.py
+++ b/solution.py
@@ -81,7 +81,7 @@
     partial_gram = jnp.dot(
         whole.T, whole, precision=lax.Precision.HIGHEST, preferred_element_type=jnp.float32
     )
-    gram = lax.psum(partial_gram, ROWS) / kept_total
+    gram = lax.psum(lax.psum(partial_gram, ("rows_1", "rows_2")), "rows_0") / kept_total
     factor = jnp.linalg.cholesky(gram).T
     return (sketch, lax.dynamic_slice_in_dim(factor, column * widths, widths, 1))
 

time: 541 us -> 494 us (0.913)
  waiting for transfers between devices: 372 us -> 326 us
    psum x1 -> x2, waiting for transfers between devices: 223 us -> 176 us  [the longest x1 98.2 us: body(): lax.psum(partial_gram, ('rows_1', 'rows_2'))]
  transfers between devices with their start and end apart: 4 -> 5, of which waited for: 4 -> 5; matrix products, arithmetic and copies ran while one was open for 0% -> 0% of each run, Pallas kernels for 0% -> 0%
where the time goes in v1:
time: 494 us
  waiting for transfers between devices  326 us (66%)
  other arithmetic  101 us (20%)
  local copies, waits for them, and re-layouts  39.6 us (8%)
  between operations  16.6 us (3%)
  matrix products  6.71 us (1%)
    reduce_scatter x3, waiting for transfers between devices, sum_by_axis(): so_far = lax.psum_scatter(so_far, axis, scatter_dimension=0, tiled=True)  149 us
    psum x1, waiting for transfers between devices, body(): lax.psum(partial_gram, ('rows_1', 'rows_2'))  98.2 us
    another operation x14, other arithmetic, body(): factor = jnp.linalg.cholesky(gram).T  78.6 us
    psum x1, waiting for transfers between devices, body(): lax.psum(lax.psum(partial_gram, ('rows_1', 'rows_2')), 'rows_0')  77.8 us
    gather x1, local copies, waits for them, and re-layouts, signed_rows(): return jnp.take(transformed, offsets, axis=0) * factor[:, None]  31.4 us
    mul x1, other arithmetic, signed_rows(): return jnp.take(transformed, offsets, axis=0) * factor[:, None]  9.89 us
  transfers between devices with their start and end apart: 5, of which 5 were waited for; matrix products, arithmetic and copies ran while one was open for 0% of the time, Pallas kernels for 0%

profile of v1, /device:TPU:2, one launch (start us, length us, event | category | flops | bytes accessed | tf_op | source)
XLA Modules:
  0.0 493.6 jit_solution(15989390673865188756)
XLA Ops:
  7.2 0.8 broadcast_multiply_fusion.7
  8.2 0.8 broadcast_multiply_fusion.6
  9.1 0.8 broadcast_clamp_fusion
  9.9 0.8 compare_and_fusion
  10.7 0.7 convert_element_type.6
  11.4 0.8 broadcast_multiply_fusion.5
  12.2 0.8 broadcast_multiply_fusion.4
  13.0 0.1 mul.277
  13.1 0.9 broadcast_multiply_fusion.2
  14.0 0.6 mul.281
  14.7 3.0 broadcast_multiply_fusion
  17.7 4.0 reshape.195
  21.7 0.2 broadcast_multiply_fusion.3
  21.9 1.8 convolution_bitcast_fusion
  23.7 0.5 copy.15
  24.2 1.0 fusion.21
  25.2 0.3 copy.16
  25.6 31.4 %gather_fusion = f32[8192,256]{1,0:T(8,128)} fusion(f32[1024,256]{1,0:T(8,128)S(1)} %bitcast.45, s32[8192]{0:T(1024)S(1)} %broadcast_clamp_fusion), kind=kCustom, calls=%fused_computation | custom fusion | bytes 16809984 | tf_op jit(solution)/shard_map/jit(_take)/gather | solution.py:66
  57.0 9.9 %select_multiply_fusion = f32[8192,256]{1,0:T(8,128)} fusion(f32[8192,256]{1,0:T(8,128)} %gather_fusion, f32[8192]{0:T(1024)S(1)} %fusion.19, pred[8192]{0:T(1024)(128)(4,1)S(1)} %compare_and_fusion), kind=kLoop, calls=%fused_computation.1 | loop fusion | flops 4194304 | bytes 16818176 | tf_op jit(solution)/shard_map/mul | solution.py:66
  66.9 97.9 %reduce-scatter.4.cloned.1.call-done = f32[1024,256]{1,0:T(8,128)} async-done(((f32[8192,256]{1,0:T(8,128)}), f32[1024,256]{1,0:T(8,128)}) %reduce-scatter.4.cloned.1.call-update) | async-done | bytes 1048592 | tf_op jit(solution)/shard_map/reduce_scatter | solution.py:13
  165.0 27.3 %reduce-scatter.6.cloned.1.call-done = f32[256,256]{1,0:T(8,128)} async-done(((f32[1024,256]{1,0:T(8,128)}), f32[256,256]{1,0:T(8,128)}) %reduce-scatter.6.cloned.1.call-update) | async-done | bytes 262160 | tf_op jit(solution)/shard_map/reduce_scatter | solution.py:13
  192.3 24.3 %reduce-scatter.8.cloned.1.call-done = f32[64,256]{1,0:T(8,128)} async-done(((f32[256,256]{1,0:T(8,128)}), f32[64,256]{1,0:T(8,128)}) %reduce-scatter.8.cloned.1.call-update) | async-done | bytes 65552 | tf_op jit(solution)/shard_map/reduce_scatter | solution.py:13
  216.6 0.8 broadcast_in_dim.59
  217.4 3.8 all_to_all.5
  221.3 2.1 fusion.22
  223.4 0.2 all-reduce.6.cloned.1.call-start
  223.6 98.2 %all-reduce.4.cloned.1.call-done = f32[512,512]{0,1:T(8,128)} async-done(((f32[512,512]{0,1:T(8,128)}), f32[512,512]{0,1:T(8,128)}) %all-reduce.4.cloned.1.call-update) | async-done | bytes 1048592 | tf_op jit(solution)/shard_map/psum | solution.py:84
  321.8 77.8 %all-reduce.6.cloned.1.call-done = f32[512,512]{0,1:T(8,128)} async-done(((f32[512,512]{0,1:T(8,128)}), f32[512,512]{0,1:T(8,128)}) %all-reduce.6.cloned.1.call-update) | async-done | bytes 1048592 | tf_op jit(solution)/shard_map/psum | solution.py:84
  399.6 1.3 broadcast_multiply_fusion.1
  401.0 0.3 copy.19
  401.3 1.5 fusion
  402.8 11.7 %cholesky.104 = f32[128,128]{1,0:T(8,128)S(1)} custom-call(f32[128,128]{1,0:T(8,128)S(1)} %cholesky.266), custom_call_target="Cholesky" | custom-call | tf_op jit(solution)/shard_map/jit(cholesky)/cholesky | solution.py:85
  414.7 9.8 %custom-call.27 = f32[1,128,128]{1,2,0:T(8,128)S(1)} custom-call(f32[1,128,128]{2,1,0:T(8,128)S(1)} %get-tuple-element.17), custom_call_target="InvertDiagBlocksLowerTriangular" | custom-call | tf_op jit(solution)/shard_map/jit(cholesky)/cholesky | solution.py:85
  424.5 0.3 constant_dynamic-update-slice_fusion.1
  424.8 0.3 convolution_subtract_fusion
  425.1 11.7 %cholesky.217 = f32[128,128]{1,0:T(8,128)S(1)} custom-call(f32[128,128]{1,0:T(8,128)S(1)} %cholesky.270), custom_call_target="Cholesky" | custom-call | tf_op jit(solution)/shard_map/jit(cholesky)/cholesky | solution.py:85
  436.9 10.0 %custom-call.28 = f32[1,128,128]{1,2,0:T(8,128)S(1)} custom-call(f32[1,128,128]{2,1,0:T(8,128)S(1)} %get-tuple-element.14), custom_call_target="InvertDiagBlocksLowerTriangular" | custom-call | tf_op jit(solution)/shard_map/jit(cholesky)/cholesky | solution.py:85
  446.9 0.3 convolution_dynamic-update-slice_fusion
  447.2 0.4 convolution_subtract_fusion.1
  447.6 11.7 %cholesky.238 = f32[128,128]{1,0:T(8,128)S(1)} custom-call(f32[128,128]{1,0:T(8,128)S(1)} %cholesky.275), custom_call_target="Cholesky" | custom-call | tf_op jit(solution)/shard_map/jit(cholesky)/cholesky | solution.py:85
  459.3 9.8 %custom-call.29 = f32[1,128,128]{1,2,0:T(8,128)S(1)} custom-call(f32[1,128,128]{2,1,0:T(8,128)S(1)} %get-tuple-element.11), custom_call_target="InvertDiagBlocksLowerTriangular" | custom-call | tf_op jit(solution)/shard_map/jit(cholesky)/cholesky | solution.py:85
  469.1 0.2 convolution_dynamic-update-slice_fusion.1
  469.4 0.4 convolution_subtract_fusion.2
  469.7 11.7 %cholesky.255 = f32[128,128]{1,0:T(8,128)S(1)} custom-call(f32[128,128]{1,0:T(8,128)S(1)} %convolution_subtract_fusion.2), custom_call_target="Cholesky" | custom-call | tf_op jit(solution)/shard_map/jit(cholesky)/cholesky | solution.py:85
  481.5 0.7 compare_reduce_fusion.1
  482.2 0.6 compare_reduce_fusion
  482.8 0.7 compare_reduce_fusion.2
  486.1 1.0 copy.20
  (28 shorter events, 1.0 us)
Async XLA Ops:
  7.2 14.5 %copy-start = (f32[1024,256]{1,0:T(8,128)S(1)}, f32[1024,256]{1,0:T(8,128)}, u32[]{:S(2)}) copy-start(f32[1024,256]{1,0:T(8,128)} %param.5) | copy-start | bytes 3145732
  7.2 157.7 %reduce-scatter.4.cloned.1.call-start = ((), (), s32[]{:S(2)}) async-start(), calls=%async_computation.4 | async-start | bytes 9437184 | tf_op jit(solution)/shard_map/reduce_scatter | solution.py:13
  17.7 7.9 %copy-start.1 = (s32[8192]{0:T(1024)S(1)}, s32[8192]{0:T(1024)}, u32[]{:S(2)}) copy-start(s32[8192]{0:T(1024)} %param.7) | copy-start | bytes 98308
  66.9 125.3 %reduce-scatter.6.cloned.1.call-start = ((), (), s32[]{:S(2)}) async-start(), calls=%async_computation.5 | async-start | bytes 1310720 | tf_op jit(solution)/shard_map/reduce_scatter | solution.py:13
  164.9 51.7 %reduce-scatter.8.cloned.1.call-start = ((), (), s32[]{:S(2)}) async-start(), calls=%async_computation.6 | async-start | bytes 327680 | tf_op jit(solution)/shard_map/reduce_scatter | solution.py:13
  192.3 129.5 %all-reduce.4.cloned.1.call-start = ((), (), s32[]{:S(2)}) async-start(), calls=%async_computation.7 | async-start | bytes 2097152 | tf_op jit(solution)/shard_map/psum | solution.py:84
  223.4 176.3 %all-reduce.6.cloned.1.call-start = ((), (), s32[]{:S(2)}) async-start(), calls=%async_computation.8 | async-start | bytes 2097152 | tf_op jit(solution)/shard_map/psum | solution.py:84
Sparse Core Ops, SparseCore 0:
  67.0 97.8 reduce-scatter.3
  167.4 24.7 reduce-scatter.5
  195.5 21.0 reduce-scatter.7
  223.5 98.2 all-reduce.3
  324.0 75.6 all-reduce.5
